TPU v7x, 256 devices: a whole 4x4x8 slice. The times are simulated.
256 devices in a mesh: leaf: 64 (over y, z, core), front: 4 (over x).
Axes of the slice: x: 4, y: 4, z: 8, core: 2. Of those that a mesh axis runs over, the one named last changes fastest.
Arguments:
- rhs_sub: float32 [8, 524288], P(None, ('leaf', 'front')), may hold values from -6 to 6
- rhs_sep: float32 [8, 16384], P(None, 'leaf'), may hold values from -6 to 6
- live_rows: int32 [256], P(('leaf', 'front')), may hold values from 256 to 2048, as said below
- lower_inv: bfloat16 [2048, 256, 256], P(('leaf', 'front')), as said below
- upper_inv: bfloat16 [2048, 256, 256], P(('leaf', 'front'))
- couple_low: bfloat16 [16384, 16384], P(('leaf', 'front')), may hold values from -0.1875 to 0.1875
- couple_up: bfloat16 [16384, 16384], P(('leaf', 'front')), may hold values from -0.046875 to 0.046875
- sep_lower_inv: bfloat16 [16384, 16384], P('leaf', 'front')
- sep_upper_inv: bfloat16 [16384, 16384], P('leaf', 'front')
- basis_sub: float32 [48, 524288], P(None, ('leaf', 'front')), may hold values from -0.0078125 to 0.0078125
- basis_sep: float32 [48, 16384], P(None, 'leaf'), may hold values from -0.0078125 to 0.0078125
Outputs:
- orth_sub: float32 [8, 524288], P(None, ('leaf', 'front'))
- orth_sep: float32 [8, 16384], P(None, 'leaf')
- coef: float32 [48, 8], replicated
Inputs may be any that keep to these rules, and one draw needn't show every extreme that they name: `live_rows`: each entry is a multiple of 256; some device has all 2048 rows live. Every block of lower_inv is lower triangular, and every block of upper_inv, sep_lower_inv and sep_upper_inv upper triangular, each with a diagonal between 1 and 1.5.
All inputs are finite; a program needn't handle non-finite values.
Results may differ from a plain program's by a relative error of at most 0.0055.
Values may be sent and summed in bfloat16 or wider, within the bound.
No kernel may reach another device: no remote copies, remote signals or barrier semaphores. Data moves between devices by JAX's collectives and lax.ppermute only.
A program may use at most 64 MiB of HBM per device.

v0:
```python
import jax
import jax.numpy as jnp
from jax import lax
from jax.sharding import PartitionSpec as P


def apply_blocks(vectors, inverse):
    vec_count = vectors.shape[0]
    shaped = vectors.astype(jnp.bfloat16).reshape(vec_count, inverse.shape[0], inverse.shape[1])
    product = jnp.einsum("vkr,krc->vkc", shaped, inverse, preferred_element_type=jnp.float32)
    return product.reshape(vec_count, inverse.shape[0] * inverse.shape[2])


def shards(
    rhs_sub,
    rhs_sep,
    live_rows,
    lower_inv,
    upper_inv,
    couple_low,
    couple_up,
    sep_lower_inv,
    sep_upper_inv,
    basis_sub,
    basis_sep,
):
    vec_count, row_count = rhs_sub.shape
    border = couple_low.shape[0]
    high = lax.Precision.HIGHEST
    live_mask = lax.broadcasted_iota(jnp.int32, (1, row_count), 1) < live_rows[0]
    lower_sol = jnp.where(live_mask, apply_blocks(rhs_sub, lower_inv), 0.0)
    border_rows = lower_sol[:, :border].astype(jnp.bfloat16)
    columns = couple_low
    top_block = lax.psum_scatter(
        lax.dot_general(
            columns, border_rows, (((0,), (1,)), ((), ())), preferred_element_type=jnp.float32
        ),
        "leaf",
        scatter_dimension=0,
        tiled=True,
    )
    top_block = lax.psum(top_block, "front")
    top_rhs = rhs_sep - top_block.T
    lower_part = jnp.dot(
        top_rhs.astype(jnp.bfloat16), sep_lower_inv, preferred_element_type=jnp.float32
    )
    top_lower = lax.psum(lower_part, "leaf")
    upper_part = lax.dot_general(
        top_lower.astype(jnp.bfloat16),
        sep_upper_inv,
        (((1,), (1,)), ((), ())),
        preferred_element_type=jnp.float32,
    )
    top_sol = lax.psum(upper_part, "front")
    columns = couple_up
    correction = lax.dot_general(
        lax.all_gather(top_sol.astype(jnp.bfloat16), "leaf", axis=1, tiled=True),
        columns,
        (((1,), (1,)), ((), ())),
        preferred_element_type=jnp.float32,
    )
    updated = jnp.concatenate([lower_sol[:, :border] - correction, lower_sol[:, border:]], axis=1)
    upper_sol = jnp.where(live_mask, apply_blocks(updated, upper_inv), 0.0)
    coef_sum = jnp.zeros((basis_sub.shape[0], vec_count), jnp.float32)
    for sweep in range(2):
        local_sub = lax.dot_general(basis_sub, upper_sol, (((1,), (1,)), ((), ())), precision=high)
        local_sep = lax.dot_general(basis_sep, top_sol, (((1,), (1,)), ((), ())), precision=high)
        coef_pass = lax.psum(local_sub, ("leaf", "front")) + lax.psum(local_sep, "leaf")
        part_sub = upper_sol
        part_sep = top_sol
        part_sub = part_sub - lax.dot_general(
            coef_pass, basis_sub, (((0,), (0,)), ((), ())), precision=high
        )
        part_sep = part_sep - lax.dot_general(
            coef_pass, basis_sep, (((0,), (0,)), ((), ())), precision=high
        )
        upper_sol = part_sub
        top_sol = part_sep
        coef_sum = coef_sum + coef_pass
    return (upper_sol, top_sol, coef_sum)


def solution(mesh):
    return jax.shard_map(
        shards,
        mesh=mesh,
        in_specs=(
            P(None, ("leaf", "front")),
            P(None, "leaf"),
            P(("leaf", "front")),
            P(("leaf", "front"), None, None),
            P(("leaf", "front"), None, None),
            P(("leaf", "front"), None),
            P(("leaf", "front"), None),
            P("leaf", "front"),
            P("leaf", "front"),
            P(None, ("leaf", "front")),
            P(None, "leaf"),
        ),
        out_specs=(P(None, ("leaf", "front")), P(None, "leaf"), P()),
        check_vma=False,
    )
```

profile of v0, /device:TPU:0, one launch (start us, length us, event | category | flops | bytes accessed | tf_op | source)
XLA Modules:
  0.0 882.8 jit_solution(9728875847282663332)
XLA Ops:
  7.2 0.0 copy-start
  7.2 0.0 reduce-scatter.2.cloned.1.call-start
  8.0 0.8 convert_element_type.20
  8.9 0.0 copy-start.6
  8.9 1.5 fusion.10
  10.4 0.0 copy-done
  10.4 0.0 copy-start.4
  10.4 1.2 convolution_bitcast_fusion
  11.6 0.0 reduce-scatter.2.cloned.1.call-update
  11.6 0.7 slice.16
  12.3 141.0 %reduce-scatter.2.cloned.1.call-done = f32[256,8]{0,1:T(8,128)} async-done(((f32[16384,8]{0,1:T(8,128)}), f32[256,8]{0,1:T(8,128)}) %reduce-scatter.2.cloned.1.call-update) | async-done | bytes 8208 | tf_op jit(solution)/shard_map/reduce_scatter | solution.py:34
  153.3 0.0 copy-done.4
  153.3 10.6 %psum.49 = f32[8,256]{1,0:T(8,128)S(1)} all-reduce(f32[8,256]{1,0:T(8,128)} %bitcast.49), channel_id=1, replica_groups=mesh['leaf'=64,'front'=4] {'front'}, use_global_device_ids=true, to_apply=%region_1.2 | all-reduce | flops 2048 | bytes 16384 | tf_op jit(solution)/shard_map/psum | solution.py:42
  163.9 0.0 copy-done.6
  163.9 2.0 fusion.6
  165.9 246.2 %all-reduce.1 = bf16[8,4096]{1,0:T(8,128)(2,1)S(1)} all-reduce(f32[8,4096]{1,0:T(8,128)S(1)} %fusion.6), channel_id=1, replica_groups=mesh['leaf'=64,'front'=4] {'leaf'}, use_global_device_ids=true, to_apply=%region_2.3 | all-reduce | flops 32768 | bytes 196608 | tf_op jit(solution)/shard_map/psum | solution.py:47
  412.0 0.0 copy-start.2
  412.0 2.9 fusion.12
  415.0 0.0 copy-start.1
  415.0 7.9 psum.51
  422.9 0.0 copy-start.5
  423.0 41.0 %all_gather.3 = bf16[8,16384]{1,0:T(8,128)(2,1)S(1)} all-gather(bf16[8,256]{1,0:T(8,128)(2,1)S(1)} %convert_element_type.24), channel_id=1, replica_groups=mesh['leaf'=64,'front'=4] {'leaf'}, dimensions={1}, use_global_device_ids=true | all-gather | bytes 266240 | tf_op jit(solution)/shard_map/all_gather | solution.py:57
  463.9 2.2 fusion
  466.2 0.0 copy-done.5
  466.2 0.1 pad_maximum_fusion
  466.3 0.0 copy-done.2
  466.3 0.2 fusion.11
  466.5 0.0 copy-start.3
  466.5 0.6 copy-done.3
  467.2 0.0 copy-done.1
  467.2 0.4 convolution_bitcast_fusion.4
  467.6 75.8 %psum.52 = f32[48,8]{0,1:T(8,128)S(1)} all-reduce(f32[48,8]{0,1:T(8,128)S(1)} %convolution_bitcast_fusion.4), channel_id=1, replica_groups=mesh['leaf'=64,'front'=4] {'leaf','front'}, use_global_device_ids=true, to_apply=%region_4.5 | all-reduce | flops 384 | bytes 3072 | tf_op jit(solution)/shard_map/psum | solution.py:68
  543.4 0.9 convolution_bitcast_fusion.2
  544.4 126.2 %psum.53 = f32[48,8]{0,1:T(8,128)S(1)} all-reduce(f32[48,8]{0,1:T(8,128)S(1)} %convolution_bitcast_fusion.2), channel_id=1, replica_groups=mesh['leaf'=64,'front'=4] {'leaf'}, use_global_device_ids=true, to_apply=%region_5.6 | all-reduce | flops 384 | bytes 3072 | tf_op jit(solution)/shard_map/psum | solution.py:68
  670.6 1.1 convolution_subtract_fusion.1
  671.7 0.9 convolution_subtract_fusion.3
  672.6 0.4 convolution_bitcast_fusion.3
  673.1 71.6 %psum.54 = f32[48,8]{0,1:T(8,128)S(1)} all-reduce(f32[48,8]{0,1:T(8,128)S(1)} %convolution_bitcast_fusion.3), channel_id=1, replica_groups=mesh['leaf'=64,'front'=4] {'leaf','front'}, use_global_device_ids=true, to_apply=%region_6.7 | all-reduce | flops 384 | bytes 3072 | tf_op jit(solution)/shard_map/psum | solution.py:68
  744.7 0.9 convolution_bitcast_fusion.1
  745.6 127.3 %psum.55 = f32[48,8]{0,1:T(8,128)S(1)} all-reduce(f32[48,8]{0,1:T(8,128)S(1)} %convolution_bitcast_fusion.1), channel_id=1, replica_groups=mesh['leaf'=64,'front'=4] {'leaf'}, use_global_device_ids=true, to_apply=%region_7.8 | all-reduce | flops 384 | bytes 3072 | tf_op jit(solution)/shard_map/psum | solution.py:68
  872.9 0.6 add_add_fusion
  873.5 1.5 convolution_subtract_fusion.2
  875.0 0.9 convolution_subtract_fusion
  (4 shorter events, 0.0 us)
Async XLA Ops:
  7.2 3.2 copy-start
  7.2 146.1 %reduce-scatter.2.cloned.1.call-start = ((), (), s32[]{:S(2)}) async-start(), calls=%async_computation.1 | async-start | bytes 532480 | tf_op jit(solution)/shard_map/reduce_scatter | solution.py:34
  8.9 155.0 %copy-start.6 = (f32[8,256]{1,0:T(8,128)S(1)}, f32[8,256]{1,0:T(8,128)}, u32[]{:S(2)}) copy-start(f32[8,256]{1,0:T(8,128)} %param.12) | copy-start | bytes 24580
  10.4 142.9 %copy-start.4 = (f32[8,2048]{1,0:T(8,128)}, f32[8,2048]{1,0:T(8,128)S(1)}, u32[]{:S(2)}) copy-start(f32[8,2048]{1,0:T(8,128)S(1)} %broadcast_select_fusion) | copy-start | bytes 196612
  412.0 54.2 %copy-start.2 = (bf16[8,256,256]{2,1,0:T(8,128)(2,1)S(1)}, bf16[8,256,256]{2,1,0:T(8,128)(2,1)}, u32[]{:S(2)}) copy-start(bf16[8,256,256]{2,1,0:T(8,128)(2,1)} %param.15) | copy-start | bytes 3145732
  415.0 52.2 %copy-start.1 = (f32[48,2048]{1,0:T(8,128)S(1)}, f32[48,2048]{1,0:T(8,128)}, u32[]{:S(2)}) copy-start(f32[48,2048]{1,0:T(8,128)} %param.20) | copy-start | bytes 1179652
  422.9 43.3 %copy-start.5 = (bf16[8,1984]{1,0:T(8,128)(2,1)S(1)}, bf16[8,1984]{1,0:T(8,128)(2,1)}, u32[]{:S(2)}) copy-start(bf16[8,1984]{1,0:T(8,128)(2,1)} %slice.16) | copy-start | bytes 95236
  466.5 0.6 copy-start.3
Sparse Core Ops, SparseCore 0:
  11.9 141.2 reduce-scatter.1
where the time goes:
time: 884 us; the launch traced here: 883 us
  blocking collectives  707 us (80%)
  waiting for transfers between devices  141 us (16%)
  matrix products  17.3 us (2%)
  between operations  14.9 us (2%)
    psum x2, blocking collectives, shards(): lax.psum(local_sep, 'leaf')  253 us
    psum x1, blocking collectives, shards(): top_lower = lax.psum(lower_part, 'leaf')  246 us
    psum x2, blocking collectives, shards(): lax.psum(local_sub, ('leaf', 'front')) + lax.psum(local_sep, 'leaf')  147 us
    reduce_scatter x1, waiting for transfers between devices, shards(): lax.psum_scatter(lax.dot_general(columns, border_rows, (((0,), (1,)), (()...  141 us
    all_gather x1, blocking collectives, shards(): lax.all_gather(top_sol.astype(jnp.bfloat16), 'leaf', axis=1, tiled=True)  41 us
  transfers between devices with their start and end apart: 1, of which 1 were waited for; matrix products, arithmetic and copies ran while one was open for 0% of the time, Pallas kernels for 0%

commit v1 on v0

--- a/solution.py
+++ b/solution.py
@@ -65,7 +65,12 @@
     for sweep in range(2):
         local_sub = lax.dot_general(basis_sub, upper_sol, (((1,), (1,)), ((), ())), precision=high)
         local_sep = lax.dot_general(basis_sep, top_sol, (((1,), (1,)), ((), ())), precision=high)
-        coef_pass = lax.psum(local_sub, ("leaf", "front")) + lax.psum(local_sep, "leaf")
+
+        def choose_joints(t0):
+            x_next = jnp.sum(lax.all_gather(t0, ("leaf", "front")), axis=0)
+            return x_next
+
+        coef_pass = choose_joints(local_sub) + lax.psum(local_sep, "leaf")
         part_sub = upper_sol
         part_sep = top_sol
         part_sub = part_sub - lax.dot_general(

time: 884 us -> 944 us (1.068)
  blocking collectives: 707 us -> 766 us
    all_gather x0 -> x2, blocking collectives: none -> 203 us  [choose_joints(): x_next = jnp.sum(lax.all_gather(t0, ('leaf', 'front')), axis=0)]
    psum x4 -> x2, blocking collectives: 401 us -> 257 us  [shards(): coef_pass = choose_joints(local_sub) + lax.psum(local_sep, 'leaf')]
where the time goes in v1:
time: 944 us; the launch traced here: 943 us
  blocking collectives  766 us (81%)
  waiting for transfers between devices  141 us (15%)
  matrix products  17.3 us (2%)
  between operations  14.9 us (2%)
    psum x2, blocking collectives, shards(): coef_pass = choose_joints(local_sub) + lax.psum(local_sep, 'leaf')  257 us
    psum x1, blocking collectives, shards(): top_lower = lax.psum(lower_part, 'leaf')  246 us
    all_gather x2, blocking collectives, choose_joints(): x_next = jnp.sum(lax.all_gather(t0, ('leaf', 'front')), axis=0)  203 us
    reduce_scatter x1, waiting for transfers between devices, shards(): lax.psum_scatter(lax.dot_general(columns, border_rows, (((0,), (1,)), (()...  141 us
    all_gather x1, blocking collectives, shards(): lax.all_gather(top_sol.astype(jnp.bfloat16), 'leaf', axis=1, tiled=True)  41 us
  transfers between devices with their start and end apart: 1, of which 1 were waited for; matrix products, arithmetic and copies ran while one was open for 0% of the time, Pallas kernels for 0%

profile of v1, /device:TPU:0, one launch (start us, length us, event | category | flops | bytes accessed | tf_op | source)
XLA Modules:
  0.0 943.4 jit_solution(285065090663142741)
XLA Ops:
  7.2 0.0 copy-start
  7.2 0.0 reduce-scatter.2.cloned.1.call-start
  8.0 0.8 convert_element_type.20
  8.9 0.0 copy-start.10
  8.9 1.5 fusion.10
  10.4 0.0 copy-done
  10.4 0.0 copy-start.6
  10.4 1.2 convolution_bitcast_fusion
  11.6 0.0 reduce-scatter.2.cloned.1.call-update
  11.6 0.7 slice.16
  12.3 141.0 %reduce-scatter.2.cloned.1.call-done = f32[256,8]{0,1:T(8,128)} async-done(((f32[16384,8]{0,1:T(8,128)}), f32[256,8]{0,1:T(8,128)}) %reduce-scatter.2.cloned.1.call-update) | async-done | bytes 8208 | tf_op jit(solution)/shard_map/reduce_scatter | solution.py:34
  153.3 0.0 copy-done.6
  153.3 10.6 %psum.35 = f32[8,256]{1,0:T(8,128)S(1)} all-reduce(f32[8,256]{1,0:T(8,128)} %bitcast.53), channel_id=1, replica_groups=mesh['leaf'=64,'front'=4] {'front'}, use_global_device_ids=true, to_apply=%region_1.2 | all-reduce | flops 2048 | bytes 16384 | tf_op jit(solution)/shard_map/psum | solution.py:42
  163.9 0.0 copy-done.10
  163.9 2.0 fusion.6
  165.9 246.2 %all-reduce.1 = bf16[8,4096]{1,0:T(8,128)(2,1)S(1)} all-reduce(f32[8,4096]{1,0:T(8,128)S(1)} %fusion.6), channel_id=1, replica_groups=mesh['leaf'=64,'front'=4] {'leaf'}, use_global_device_ids=true, to_apply=%region_2.3 | all-reduce | flops 32768 | bytes 196608 | tf_op jit(solution)/shard_map/psum | solution.py:47
  412.0 2.9 fusion.12
  415.0 7.9 psum.37
  422.9 0.0 copy-start.7
  423.0 41.0 %all_gather.15 = bf16[8,16384]{1,0:T(8,128)(2,1)S(1)} all-gather(bf16[8,256]{1,0:T(8,128)(2,1)S(1)} %convert_element_type.24), channel_id=1, replica_groups=mesh['leaf'=64,'front'=4] {'leaf'}, dimensions={1}, use_global_device_ids=true | all-gather | bytes 266240 | tf_op jit(solution)/shard_map/all_gather | solution.py:57
  464.0 2.2 fusion
  466.2 0.0 copy-done.7
  466.2 0.1 pad_maximum_fusion
  466.3 0.0 copy-done.2
  466.3 0.2 fusion.11
  466.5 0.6 copy-done.4
  467.2 0.0 copy-done.1
  467.2 0.4 convolution_bitcast_fusion.4
  467.6 102.5 %all-gather.2 = f32[256,48,8]{1,2,0:T(8,128)S(1)} all-gather(f32[1,48,8]{1,2,0:T(8,128)S(1)} %convolution_bitcast_fusion.4), channel_id=2, replica_groups=mesh['leaf'=64,'front'=4] {'leaf','front'}, dimensions={0}, use_global_device_ids=true | all-gather | bytes 394752 | tf_op jit(solution)/shard_map/all_gather | solution.py:70
  570.1 0.0 copy-done.3
  570.1 0.1 convolution_bitcast_fusion.2
  570.2 128.8 %psum.38 = f32[48,8]{0,1:T(8,128)} all-reduce(f32[48,8]{0,1:T(8,128)S(1)} %convolution_bitcast_fusion.2), channel_id=1, replica_groups=mesh['leaf'=64,'front'=4] {'leaf'}, use_global_device_ids=true, to_apply=%region_5.6 | all-reduce | flops 384 | bytes 3072 | tf_op jit(solution)/shard_map/psum | solution.py:73
  699.1 0.3 reduce_sum.18
  699.3 0.7 add.21
  700.0 1.1 convolution_subtract_fusion.1
  701.2 0.0 copy-start.5
  701.2 1.0 convolution_subtract_fusion.3
  702.2 0.0 copy-done.8
  702.2 0.0 copy-done.5
  702.2 0.4 convolution_bitcast_fusion.3
  702.6 100.6 %all-gather.3 = f32[256,48,8]{1,2,0:T(8,128)S(1)} all-gather(f32[1,48,8]{1,2,0:T(8,128)S(1)} %convolution_bitcast_fusion.3), channel_id=3, replica_groups=mesh['leaf'=64,'front'=4] {'leaf','front'}, dimensions={0}, use_global_device_ids=true | all-gather | bytes 394752 | tf_op jit(solution)/shard_map/all_gather | solution.py:70
  803.2 0.3 reduce_sum.19
  803.5 0.9 convolution_bitcast_fusion.1
  804.4 128.3 %psum.39 = f32[48,8]{0,1:T(8,128)S(1)} all-reduce(f32[48,8]{0,1:T(8,128)S(1)} %convolution_bitcast_fusion.1), channel_id=1, replica_groups=mesh['leaf'=64,'front'=4] {'leaf'}, use_global_device_ids=true, to_apply=%region_7.8 | all-reduce | flops 384 | bytes 3072 | tf_op jit(solution)/shard_map/psum | solution.py:73
  932.7 0.0 copy-done.9
  932.7 0.6 add_add_fusion
  933.3 1.5 convolution_subtract_fusion.2
  934.8 1.8 convolution_subtract_fusion
  (9 shorter events, 0.0 us)
Async XLA Ops:
  7.2 3.2 copy-start
  7.2 146.1 %reduce-scatter.2.cloned.1.call-start = ((), (), s32[]{:S(2)}) async-start(), calls=%async_computation.1 | async-start | bytes 532480 | tf_op jit(solution)/shard_map/reduce_scatter | solution.py:34
  8.9 155.0 %copy-start.10 = (f32[8,256]{1,0:T(8,128)S(1)}, f32[8,256]{1,0:T(8,128)}, u32[]{:S(2)}) copy-start(f32[8,256]{1,0:T(8,128)} %param.12) | copy-start | bytes 24580
  10.4 142.9 %copy-start.6 = (f32[8,2048]{1,0:T(8,128)}, f32[8,2048]{1,0:T(8,128)S(1)}, u32[]{:S(2)}) copy-start(f32[8,2048]{1,0:T(8,128)S(1)} %broadcast_select_fusion) | copy-start | bytes 196612
  412.0 54.2 %copy-start.2 = (bf16[8,256,256]{2,1,0:T(8,128)(2,1)S(1)}, bf16[8,256,256]{2,1,0:T(8,128)(2,1)}, u32[]{:S(2)}) copy-start(bf16[8,256,256]{2,1,0:T(8,128)(2,1)} %param.15) | copy-start | bytes 3145732
  415.0 52.2 %copy-start.1 = (f32[48,2048]{1,0:T(8,128)S(1)}, f32[48,2048]{1,0:T(8,128)}, u32[]{:S(2)}) copy-start(f32[48,2048]{1,0:T(8,128)} %param.20) | copy-start | bytes 1179652
  422.9 43.3 %copy-start.7 = (bf16[8,1984]{1,0:T(8,128)(2,1)S(1)}, bf16[8,1984]{1,0:T(8,128)(2,1)}, u32[]{:S(2)}) copy-start(bf16[8,1984]{1,0:T(8,128)(2,1)} %slice.16) | copy-start | bytes 95236
  463.9 106.2 %copy-start.3 = (f32[48,256]{1,0:T(8,128)S(1)}, f32[48,256]{1,0:T(8,128)}, u32[]{:S(2)}) copy-start(f32[48,256]{1,0:T(8,128)} %param.21) | copy-start | bytes 147460
  466.5 0.6 copy-start.4
  700.0 2.1 copy-start.8
  701.2 1.0 copy-start.5
  702.6 230.1 %copy-start.9 = (f32[48,8]{0,1:T(8,128)S(1)}, f32[48,8]{0,1:T(8,128)}, u32[]{:S(2)}) copy-start(f32[48,8]{0,1:T(8,128)} %copy-done.8) | copy-start | bytes 4612
Sparse Core Ops, SparseCore 0:
  11.9 141.2 reduce-scatter.1
